TPU v7x, 32 devices: a whole 2x2x4 slice. The times are simulated.
32 devices in a mesh: dp: 16 (over z, y, x), tensor: 2 (over core).
Axes of the slice: x: 2, y: 2, z: 4, core: 2. Of those that a mesh axis runs over, the one named last changes fastest.
Arguments:
- layer_input: bfloat16 [16, 1024, 1024], P('dp', 'tensor'), may hold values from -6 to 6
- memory: bfloat16 [16, 512, 1024], P('dp', 'tensor'), may hold values from -6 to 6
- evicted: bfloat16 [16, 1536, 1024], P('dp', 'tensor'), may hold values from -6 to 6
- picture_start: int32 [16], P('dp'), may hold values from 0 to 768, as said below
- memory_lengths: int32 [16, 2], P('dp'), may hold values from 128 to 512, as said below
- w_query: bfloat16 [1024, 1024], P('dp', 'tensor'), may hold values from -0.1875 to 0.1875
- w_key: bfloat16 [1024, 1024], P('dp', 'tensor'), may hold values from -0.1875 to 0.1875
- w_value: bfloat16 [1024, 1024], P('dp', 'tensor'), may hold values from -0.1875 to 0.1875
- w_output: bfloat16 [1024, 1024], P('tensor', 'dp'), may hold values from -1.5 to 1.5
- w_compress: bfloat16 [3072, 1024], P(('dp', 'tensor')), may hold values from -0.109375 to 0.109375
- gain_attn: bfloat16 [1024], P(('dp', 'tensor')), may hold values from 0.5 to 1.5
- gain_ffn: bfloat16 [1024], P(('dp', 'tensor')), may hold values from 0.5 to 1.5
- w_inner: bfloat16 [1024, 4096], P('dp', 'tensor'), may hold values from -0.1875 to 0.1875
- w_outer: bfloat16 [4096, 1024], P('tensor', 'dp'), may hold values from -0.09375 to 0.09375
- cotangent: bfloat16 [16, 1024, 1024], P('dp', 'tensor'), may hold values from -6 to 6
Outputs:
- layer_output: bfloat16 [16, 1024, 1024], P('dp', 'tensor')
- input_grad: bfloat16 [16, 1024, 1024], P('dp', 'tensor')
- grad_query: float32 [1024, 1024], P('dp', 'tensor')
- grad_key: float32 [1024, 1024], P('dp', 'tensor')
- grad_value: float32 [1024, 1024], P('dp', 'tensor')
- grad_output_proj: float32 [1024, 1024], P('tensor', 'dp')
- grad_compress: float32 [3072, 1024], P(('dp', 'tensor'))
- grad_gain_attn: float32 [1024], P(('dp', 'tensor'))
- grad_gain_ffn: float32 [1024], P(('dp', 'tensor'))
- grad_inner: float32 [1024, 4096], P('dp', 'tensor')
- grad_outer: float32 [4096, 1024], P('tensor', 'dp')
- branch_rms: float32 [16, 3], P('dp')
Inputs may be any that keep to these rules, and one draw needn't show every extreme that they name: Sequence s treats tokens picture_start[s] to picture_start[s] + 255 as one picture span; starts are multiples of half of 256. `memory_lengths`: column 0 counts the valid most recent rows of memory, column 1 those of compressed memory.
All inputs are finite; a program needn't handle non-finite values.
Results may differ from a plain program's by a relative error of at most 0.018.
Values may be sent and summed in bfloat16 or wider, within the bound.
No kernel may reach another device: no remote copies, remote signals or barrier semaphores. Data moves between devices by JAX's collectives and lax.ppermute only.
A program may use at most 256 MiB of HBM per device.

v0:
```python
import jax
import jax.numpy as jnp
from jax import lax
from jax.sharding import PartitionSpec as P

D = 1024
DH = 128
MEM = 512
CMEM = 512
PIC = 256
L = 1024
epsilon = 1e-06
very_negative = -1e30


def rms_norm(matrix_rows, gain_vec):
    return (
        matrix_rows
        * lax.rsqrt(jnp.mean(matrix_rows * matrix_rows, axis=-1, keepdims=True) + epsilon)
        * gain_vec
    )


def allowed_keys(span_start, valid_lens):
    query_pos = jnp.arange(L, dtype=jnp.int32)[:, None]
    key_pos = jnp.arange(CMEM + MEM + L, dtype=jnp.int32)[None, :]
    comp_ok = (key_pos < CMEM) & (key_pos >= CMEM - valid_lens[1])
    mem_pos = key_pos - CMEM
    mem_ok = (mem_pos >= 0) & (mem_pos < MEM) & (mem_pos >= MEM - valid_lens[0])
    tok_pos = key_pos - CMEM - MEM
    query_pic = (query_pos >= span_start) & (query_pos < span_start + PIC)
    key_pic = (tok_pos >= span_start) & (tok_pos < span_start + PIC)
    tok_ok = (tok_pos >= 0) & ((tok_pos <= query_pos) | query_pic & key_pic)
    return comp_ok | mem_ok | tok_ok


def masked_scores(query_rows, key_rows, span_start, valid_lens):
    allowed = allowed_keys(span_start, valid_lens)
    scores = DH ** (-0.5) * jnp.einsum(
        "qhd,khd->hqk", query_rows, key_rows, preferred_element_type=jnp.float32
    )
    return jnp.where(allowed[None], scores, very_negative)


def attend_one(seq_items):
    query_rows, key_rows, value_rows, span_start, valid_lens = seq_items
    scores = masked_scores(query_rows, key_rows, span_start, valid_lens)
    row_max = jnp.max(scores, axis=-1, keepdims=True)
    shifted = jnp.exp(scores - row_max)
    row_total = jnp.sum(shifted, axis=-1, keepdims=True)
    attn_probs = (shifted / row_total).astype(jnp.bfloat16)
    mixed = jnp.einsum("hqk,khd->qhd", attn_probs, value_rows, preferred_element_type=jnp.float32)
    return (mixed.astype(jnp.bfloat16), row_max + jnp.log(row_total))


def attend_back(seq_items):
    query_rows, key_rows, value_rows, d_mixed, log_total, span_start, valid_lens = seq_items
    scores = masked_scores(query_rows, key_rows, span_start, valid_lens)
    attn_probs = jnp.exp(scores - log_total)
    d_probs = jnp.einsum("qhd,khd->hqk", d_mixed, value_rows, preferred_element_type=jnp.float32)
    d_values = jnp.einsum(
        "hqk,qhd->khd", attn_probs.astype(jnp.bfloat16), d_mixed, preferred_element_type=jnp.float32
    )
    d_scores = (
        attn_probs * (d_probs - jnp.sum(attn_probs * d_probs, axis=-1, keepdims=True))
    ).astype(jnp.bfloat16)
    query_gradient = DH ** (-0.5) * jnp.einsum(
        "hqk,khd->qhd", d_scores, key_rows, preferred_element_type=jnp.float32
    )
    d_keys = DH ** (-0.5) * jnp.einsum(
        "hqk,qhd->khd", d_scores, query_rows, preferred_element_type=jnp.float32
    )
    return (
        query_gradient.astype(jnp.bfloat16),
        d_keys.astype(jnp.bfloat16),
        d_values.astype(jnp.bfloat16),
    )


def to_natural(spread, tensor_size, comp_part, mem_part):
    seq_dev = spread.shape[0]
    feature_dim = spread.shape[-1]
    split_rows = spread.reshape(seq_dev, tensor_size, -1, feature_dim)
    comp_rows = split_rows[:, :, :comp_part].reshape(seq_dev, -1, feature_dim)
    mem_rows = split_rows[:, :, comp_part : comp_part + mem_part].reshape(seq_dev, -1, feature_dim)
    tok_rows = split_rows[:, :, comp_part + mem_part :].reshape(seq_dev, -1, feature_dim)
    return jnp.concatenate([comp_rows, mem_rows, tok_rows], axis=1)


def from_natural(natural, tensor_size, comp_part, mem_part):
    seq_dev = natural.shape[0]
    feature_dim = natural.shape[-1]
    comp_all = tensor_size * comp_part
    mem_all = tensor_size * mem_part
    comp_rows = natural[:, :comp_all].reshape(seq_dev, tensor_size, comp_part, feature_dim)
    mem_rows = natural[:, comp_all : comp_all + mem_all].reshape(
        seq_dev, tensor_size, mem_part, feature_dim
    )
    tok_rows = natural[:, comp_all + mem_all :].reshape(seq_dev, tensor_size, -1, feature_dim)
    return jnp.concatenate([comp_rows, mem_rows, tok_rows], axis=2).reshape(
        seq_dev, -1, feature_dim
    )


def gelu_tanh(inner_in):
    return jax.nn.gelu(inner_in, approximate=True)


def per_device(
    layer_input,
    memory,
    evicted,
    picture_start,
    memory_lengths,
    w_query,
    w_key,
    w_value,
    w_output,
    w_compress,
    gain_attn,
    gain_ffn,
    w_inner,
    w_outer,
    cotangent,
):
    tensor_size = lax.axis_size("tensor")
    seq_dev, part_len, feature_dim = layer_input.shape
    comp_part = evicted.shape[1] // 3
    mem_part = memory.shape[1]
    head_local = w_query.shape[1] // DH
    key_len = CMEM + MEM + L
    compress_full, gain_a_full, gain_f_full = (
        lax.all_gather(w_compress, ("dp", "tensor"), axis=0, tiled=True),
        lax.all_gather(gain_attn, ("dp", "tensor"), axis=0, tiled=True),
        lax.all_gather(gain_ffn, ("dp", "tensor"), axis=0, tiled=True),
    )
    gain_attn_f = gain_a_full.astype(jnp.float32)
    gain_ffn_f = gain_f_full.astype(jnp.float32)
    query_weight, key_w, value_w, output_weight, inner_weight, outer_weight = (
        lax.all_gather(w_query, "dp", axis=0, tiled=True),
        lax.all_gather(w_key, "dp", axis=0, tiled=True),
        lax.all_gather(w_value, "dp", axis=0, tiled=True),
        lax.all_gather(w_output, "dp", axis=1, tiled=True),
        lax.all_gather(w_inner, "dp", axis=0, tiled=True),
        lax.all_gather(w_outer, "dp", axis=1, tiled=True),
    )
    grouped = evicted.reshape(seq_dev, comp_part, 3 * feature_dim)
    compressed = jnp.einsum(
        "sce,ed->scd", grouped, compress_full, preferred_element_type=jnp.float32
    )
    token_f = layer_input.astype(jnp.float32)
    keyed_rows = jnp.concatenate([compressed, memory.astype(jnp.float32), token_f], axis=1)
    attn_value, attn_pull = jax.vjp(rms_norm, keyed_rows, gain_attn_f)
    attn_normed = attn_value.astype(jnp.bfloat16)
    spread_rows = lax.all_gather(attn_normed, "tensor", axis=1, tiled=True)
    natural_rows = to_natural(spread_rows, tensor_size, comp_part, mem_part)
    token_normalized = natural_rows[:, CMEM + MEM :]
    query_rows = jnp.einsum(
        "ujm,mk->ujk", token_normalized, query_weight, preferred_element_type=jnp.float32
    ).astype(jnp.bfloat16)
    key_rows = jnp.einsum(
        "skd,de->ske", natural_rows, key_w, preferred_element_type=jnp.float32
    ).astype(jnp.bfloat16)
    value_rows = jnp.einsum(
        "skd,de->ske", natural_rows, value_w, preferred_element_type=jnp.float32
    ).astype(jnp.bfloat16)
    query_heads = query_rows.reshape(seq_dev, L, head_local, DH)
    key_heads = key_rows.reshape(seq_dev, key_len, head_local, DH)
    value_heads = value_rows.reshape(seq_dev, key_len, head_local, DH)
    mixed_heads, log_total = lax.map(
        attend_one, (query_heads, key_heads, value_heads, picture_start, memory_lengths)
    )
    mixed_flattened = mixed_heads.reshape(seq_dev, L, head_local * DH)
    branch_part = jnp.einsum(
        "avr,ri->avi", mixed_flattened, output_weight, preferred_element_type=jnp.float32
    )
    attn_branch = lax.psum_scatter(
        branch_part.astype(jnp.bfloat16), "tensor", scatter_dimension=1, tiled=True
    ).astype(jnp.float32)
    after_attn = token_f + attn_branch
    ffn_value, ffn_pull = jax.vjp(rms_norm, after_attn, gain_ffn_f)
    ffn_normed = ffn_value.astype(jnp.bfloat16)
    feedforward_rows = lax.all_gather(ffn_normed, "tensor", axis=1, tiled=True)
    inner_hidden = jnp.einsum(
        "qmy,yx->qmx", feedforward_rows, inner_weight, preferred_element_type=jnp.float32
    )
    active_f, gelu_pull = jax.vjp(gelu_tanh, inner_hidden)
    hidden_active = active_f.astype(jnp.bfloat16)
    feedforward_share = jnp.einsum(
        "qwh,hj->qwj", hidden_active, outer_weight, preferred_element_type=jnp.float32
    )
    ffn_branch = lax.psum_scatter(
        feedforward_share.astype(jnp.bfloat16), "tensor", scatter_dimension=1, tiled=True
    ).astype(jnp.float32)
    summed = after_attn + ffn_branch
    layer_output = summed.astype(jnp.bfloat16)
    square_sums = jnp.stack(
        [
            jnp.sum(attn_branch * attn_branch, axis=(1, 2)),
            jnp.sum(ffn_branch * ffn_branch, axis=(1, 2)),
            jnp.sum(summed * summed, axis=(1, 2)),
        ],
        axis=1,
    )
    incoming_row_grads = lax.all_gather(cotangent, "tensor", axis=1, tiled=True)
    active_gradient = jnp.einsum(
        "wve,ne->wvn", incoming_row_grads, outer_weight, preferred_element_type=jnp.float32
    )
    grad_outer_part = jnp.einsum(
        "wkz,wky->zy", hidden_active, incoming_row_grads, preferred_element_type=jnp.float32
    )
    inner_gradient = gelu_pull(active_gradient)[0].astype(jnp.bfloat16)
    grad_inner_part = jnp.einsum(
        "vea,vem->am", feedforward_rows, inner_gradient, preferred_element_type=jnp.float32
    )
    feedforward_row_gradient = jnp.einsum(
        "tar,br->tab", inner_gradient, inner_weight, preferred_element_type=jnp.float32
    )
    tiled_sums = jnp.tile(square_sums, (1, tensor_size))
    d_ffn_normed, seq_sums = (
        lax.psum_scatter(
            feedforward_row_gradient.astype(jnp.bfloat16), "tensor", scatter_dimension=1, tiled=True
        ).astype(jnp.float32),
        lax.psum_scatter(
            tiled_sums.astype(jnp.bfloat16), "tensor", scatter_dimension=1, tiled=True
        ).astype(jnp.float32),
    )
    branch_rms = jnp.sqrt(seq_sums / (L * D))
    d_after, grad_gain_ffn_part = ffn_pull(d_ffn_normed)
    grad_after = cotangent.astype(jnp.float32) + d_after
    incoming_attention_grad = lax.all_gather(
        grad_after.astype(jnp.bfloat16), "tensor", axis=1, tiled=True
    )
    d_mixed = jnp.einsum(
        "gqa,ba->gqb", incoming_attention_grad, output_weight, preferred_element_type=jnp.float32
    ).astype(jnp.bfloat16)
    grad_output_part = jnp.einsum(
        "knm,knc->mc", mixed_flattened, incoming_attention_grad, preferred_element_type=jnp.float32
    )
    query_gradient, d_keys, d_values = lax.map(
        attend_back,
        (
            query_heads,
            key_heads,
            value_heads,
            d_mixed.reshape(seq_dev, L, head_local, DH),
            log_total,
            picture_start,
            memory_lengths,
        ),
    )
    query_gradient = query_gradient.reshape(seq_dev, L, head_local * DH)
    d_keys = d_keys.reshape(seq_dev, key_len, head_local * DH)
    d_values = d_values.reshape(seq_dev, key_len, head_local * DH)
    grad_query_part = jnp.einsum(
        "frk,frj->kj", token_normalized, query_gradient, preferred_element_type=jnp.float32
    )
    grad_key_part = jnp.einsum(
        "skd,ske->de", natural_rows, d_keys, preferred_element_type=jnp.float32
    )
    grad_value_part = jnp.einsum(
        "skd,ske->de", natural_rows, d_values, preferred_element_type=jnp.float32
    )
    d_natural = jnp.einsum(
        "ske,de->skd", d_keys, key_w, preferred_element_type=jnp.float32
    ) + jnp.einsum("ske,de->skd", d_values, value_w, preferred_element_type=jnp.float32)
    token_gradient = jnp.einsum(
        "iuo,co->iuc", query_gradient, query_weight, preferred_element_type=jnp.float32
    )
    d_natural = jnp.concatenate(
        [d_natural[:, : CMEM + MEM], d_natural[:, CMEM + MEM :] + token_gradient], axis=1
    )
    d_spread = from_natural(d_natural, tensor_size, comp_part, mem_part)
    d_attn_normed = lax.psum_scatter(
        d_spread.astype(jnp.bfloat16), "tensor", scatter_dimension=1, tiled=True
    ).astype(jnp.float32)
    d_keyed, grad_gain_attn_part = attn_pull(d_attn_normed)
    input_grad = (grad_after + d_keyed[:, comp_part + mem_part :]).astype(jnp.bfloat16)
    d_compressed = d_keyed[:, :comp_part].astype(jnp.bfloat16)
    grad_compress_part = jnp.einsum(
        "sce,scd->ed", grouped, d_compressed, preferred_element_type=jnp.float32
    )
    grad_compress, grad_gain_attn, grad_gain_ffn = (
        lax.psum_scatter(grad_compress_part, ("dp", "tensor"), scatter_dimension=0, tiled=True),
        lax.psum_scatter(grad_gain_attn_part, ("dp", "tensor"), scatter_dimension=0, tiled=True),
        lax.psum_scatter(grad_gain_ffn_part, ("dp", "tensor"), scatter_dimension=0, tiled=True),
    )
    grad_query, grad_key, grad_value, grad_output_proj, grad_inner, grad_outer = (
        lax.psum_scatter(grad_query_part, "dp", scatter_dimension=0, tiled=True),
        lax.psum_scatter(grad_key_part, "dp", scatter_dimension=0, tiled=True),
        lax.psum_scatter(grad_value_part, "dp", scatter_dimension=0, tiled=True),
        lax.psum_scatter(grad_output_part, "dp", scatter_dimension=1, tiled=True),
        lax.psum_scatter(grad_inner_part, "dp", scatter_dimension=0, tiled=True),
        lax.psum_scatter(grad_outer_part, "dp", scatter_dimension=1, tiled=True),
    )
    return (
        layer_output,
        input_grad,
        grad_query,
        grad_key,
        grad_value,
        grad_output_proj,
        grad_compress,
        grad_gain_attn,
        grad_gain_ffn,
        grad_inner,
        grad_outer,
        branch_rms,
    )


def solution(mesh):
    in_specs = (
        P("dp", "tensor", None),
        P("dp", "tensor", None),
        P("dp", "tensor", None),
        P("dp"),
        P("dp", None),
        P("dp", "tensor"),
        P("dp", "tensor"),
        P("dp", "tensor"),
        P("tensor", "dp"),
        P(("dp", "tensor"), None),
        P(("dp", "tensor")),
        P(("dp", "tensor")),
        P("dp", "tensor"),
        P("tensor", "dp"),
        P("dp", "tensor", None),
    )
    out_specs = (
        P("dp", "tensor", None),
        P("dp", "tensor", None),
        P("dp", "tensor"),
        P("dp", "tensor"),
        P("dp", "tensor"),
        P("tensor", "dp"),
        P(("dp", "tensor"), None),
        P(("dp", "tensor")),
        P(("dp", "tensor")),
        P("dp", "tensor"),
        P("tensor", "dp"),
        P("dp", None),
    )
    return jax.shard_map(
        per_device, mesh=mesh, in_specs=in_specs, out_specs=out_specs, check_vma=False
    )
```

profile of v0, /device:TPU:0, one launch (start us, length us, event | category | flops | bytes accessed | tf_op | source)
XLA Modules:
  0.0 1562.3 jit_solution(4644787308819729858)
XLA Ops:
  9.7 42.9 %all-reduce.6 = (bf16[1024]{0:T(1024)(128)(2,1)S(1)}, bf16[1024]{0:T(1024)(128)(2,1)S(1)}) all-reduce(bf16[1024]{0:T(1024)(128)(2,1)S(1)} %dynamic-update-slice.1, bf16[1024]{0:T(1024)(128)(2,1)S(1)} %dynamic-update-slice), channel_id=1, replica_groups=mesh['dp'=16,'tensor'=2] {'dp','tensor'}, use_global_device_ids=true, to_apply=%add.1 | all-reduce | flops 2048 | bytes 8192
  54.7 3.7 reshape.678
  58.7 24.3 %all-gather.12.cloned.1.call-done = bf16[3072,1024]{1,0:T(8,128)(2,1)} async-done(((bf16[96,1024]{1,0:T(8,128)(2,1)}), bf16[3072,1024]{1,0:T(8,128)(2,1)}) %all-gather.12.cloned.1.call-update) | async-done | bytes 6291472 | tf_op jit(solution)/shard_map/all_gather | solution.py:133
  83.0 5.1 convolution_bitcast_fusion.1
  97.2 4.2 fusion.15
  108.3 54.7 %all-gather.18.cloned.1.call-done = bf16[1024,512]{1,0:T(8,128)(2,1)} async-done(((bf16[64,512]{1,0:T(8,128)(2,1)}), bf16[1024,512]{1,0:T(8,128)(2,1)}) %all-gather.18.cloned.1.call-update) | async-done | bytes 1048592 | tf_op jit(solution)/shard_map/all_gather | solution.py:140
  163.0 3.5 convolution_convert_fusion.2
  166.5 53.1 %all-gather.20.cloned.1.call-done = bf16[1024,512]{1,0:T(8,128)(2,1)} async-done(((bf16[64,512]{1,0:T(8,128)(2,1)}), bf16[1024,512]{1,0:T(8,128)(2,1)}) %all-gather.20.cloned.1.call-update) | async-done | bytes 1048592 | tf_op jit(solution)/shard_map/all_gather | solution.py:141
  219.5 4.4 convolution_convert_fusion
  224.0 16.4 %fusion.75 = (f32[4,1024]{1,0:T(4,128)S(1)}, f32[4,1024,2048]{2,1,0:T(8,128)}) fusion(bf16[1024,4,128]{0,2,1:T(8,128)(2,1)} %bitcast.143, bf16[2048,4,128]{0,2,1:T(8,128)(2,1)S(1)} %bitcast.125, pred[1024,2048]{1,0:T(8,128)(4,1)S(1)} %copy-done.23), kind=kOutput, calls=%fused_computation.122 | convolution fusion | flops 2172645376 | bytes 38813696 | tf_op jit(solution)/shard_map/while/body/eval_jaxpr/qhd,khd->hqk/dot_general | solution.py:39
  240.4 13.8 fusion
  254.2 21.9 %all-gather.16.cloned.1.call-done = bf16[1024,512]{1,0:T(8,128)(2,1)} async-done(((bf16[64,512]{1,0:T(8,128)(2,1)}), bf16[1024,512]{1,0:T(8,128)(2,1)}) %all-gather.16.cloned.1.call-update) | async-done | bytes 1048592 | tf_op jit(solution)/shard_map/all_gather | solution.py:142
  276.1 4.9 convolution_convert_fusion.1
  281.0 15.7 %fusion.49 = bf16[4,128,1024]{2,1,0:T(8,128)(2,1)} fusion(bf16[2048,4,128]{0,2,1:T(8,128)(2,1)S(1)} %bitcast.133, f32[4,1024,2048]{2,1,0:T(8,128)} %get-tuple-element.112, f32[4,1024]{1,0:T(4,128)S(1)} %fusion, f32[4,1024]{1,0:T(4,128)S(1)} %get-tuple-element.111), kind=kOutput, calls=%fused_computation.82 | convolution fusion | flops 2173173760 | bytes 36732928 | tf_op jit(solution)/shard_map/while/body/eval_jaxpr/hqk,khd->qhd/dot_general | solution.py:52
  296.7 36.0 %all-gather.22.cloned.1.call-done = bf16[512,1024]{0,1:T(8,128)(2,1)} async-done(((bf16[512,64]{0,1:T(8,128)(2,1)}), bf16[512,1024]{0,1:T(8,128)(2,1)}) %all-gather.22.cloned.1.call-update) | async-done | bytes 1048592 | tf_op jit(solution)/shard_map/all_gather | solution.py:143
  332.7 4.2 convert_bitcast_fusion.2
  337.7 7.9 reduce-scatter.15.cloned.1.call-done
  351.2 74.1 %all-gather.26.cloned.1.call-done = bf16[1024,2048]{1,0:T(8,128)(2,1)} async-done(((bf16[64,2048]{1,0:T(8,128)(2,1)}), bf16[1024,2048]{1,0:T(8,128)(2,1)}) %all-gather.26.cloned.1.call-update) | async-done | bytes 4194320 | tf_op jit(solution)/shard_map/all_gather | solution.py:144
  425.3 11.3 all-gather.24.cloned.1.call-done
  436.6 11.0 fusion.44
  449.8 79.6 %all-gather.28.cloned.1.call-done = bf16[2048,1024]{0,1:T(8,128)(2,1)} async-done(((bf16[2048,64]{0,1:T(8,128)(2,1)}), bf16[2048,1024]{0,1:T(8,128)(2,1)}) %all-gather.28.cloned.1.call-update) | async-done | bytes 4194320 | tf_op jit(solution)/shard_map/all_gather | solution.py:145
  529.4 12.7 fusion.12
  544.1 5.8 convert_bitcast_fusion
  550.0 11.2 convert_bitcast_fusion.1
  561.6 10.1 reduce-scatter.17.cloned.1.call-done
  571.7 5.2 fusion.29
  579.4 11.9 all-gather.32.cloned.1.call-done
  591.3 3.1 fusion.46
  594.5 13.7 fusion.21
  608.3 22.0 %multiply_reduce_fusion = (f32[4,1024]{1,0:T(4,128)S(1)}, f32[4,1024,2048]{2,1,0:T(8,128)}) fusion(f32[4,1024,2048]{2,1,0:T(8,128)} %get-tuple-element.112, f32[4,1024]{1,0:T(4,128)S(1)} %log_add_fusion, bf16[1024,4,128]{0,2,1:T(8,128)(2,1)S(1)} %bitcast.128, bf16[2048,4,128]{0,2,1:T(8,128)(2,1)S(1)} %bitcast.134), kind=kOutput, calls=%fused_computation.1 | convolution fusion | flops 2172645376 | bytes 70287360 | tf_op jit(solution)/shard_map/while/body/eval_jaxpr/qhd,khd->hqk/dot_general | solution.py:60
  630.3 27.9 %multiply_convert_fusion = bf16[4,1024,2048]{2,1,0:T(8,128)(2,1)} fusion(f32[4,1024,2048]{2,1,0:T(8,128)} %get-tuple-element.114, f32[4,1024,2048]{2,1,0:T(8,128)} %get-tuple-element.112, f32[4,1024]{1,0:T(4,128)S(1)} %get-tuple-element.113, f32[4,1024]{1,0:T(4,128)S(1)} %log_add_fusion), kind=kLoop, calls=%fused_computation | loop fusion | flops 33554432 | bytes 83918848 | tf_op jit(solution)/shard_map/while/body/eval_jaxpr/convert_element_type | solution.py:66
  658.2 12.1 multiply_convert_fusion.4
  670.3 8.6 multiply_convert_fusion.2
  688.9 4.6 fusion.32
  693.6 5.9 fusion.70
  699.6 7.2 fusion.71
  709.8 12.0 fusion.36
  723.4 9.0 fusion.42
  741.2 6.4 convolution_bitcast_fusion
  747.6 12.7 copy.41
  767.3 41.1 %all-reduce.5 = (f32[1024]{0:T(1024)S(1)}, f32[1024]{0:T(1024)S(1)}) all-reduce(f32[1024]{0:T(1024)S(1)} %get-tuple-element.93, f32[1024]{0:T(1024)S(1)} %copy-done.38), channel_id=11, replica_groups=mesh['dp'=16,'tensor'=2] {'dp','tensor'}, use_global_device_ids=true, to_apply=%region_17.18.clone | all-reduce | flops 2048 | bytes 16384
  809.7 3.7 fusion.31
  813.4 55.1 %reduce-scatter.27.cloned.1.call-done = f32[64,512]{1,0:T(8,128)} async-done(((f32[1024,512]{1,0:T(8,128)}), f32[64,512]{1,0:T(8,128)}) %reduce-scatter.27.cloned.1.call-update) | async-done | bytes 131088 | tf_op jit(solution)/shard_map/reduce_scatter | solution.py:291
  868.5 81.0 %reduce-scatter.25.cloned.1.call-done = f32[64,512]{1,0:T(8,128)} async-done(((f32[1024,512]{1,0:T(8,128)}), f32[64,512]{1,0:T(8,128)}) %reduce-scatter.25.cloned.1.call-update) | async-done | bytes 131088 | tf_op jit(solution)/shard_map/reduce_scatter | solution.py:290
  949.5 81.0 %reduce-scatter.23.cloned.1.call-done = f32[64,512]{1,0:T(8,128)} async-done(((f32[1024,512]{1,0:T(8,128)}), f32[64,512]{1,0:T(8,128)}) %reduce-scatter.23.cloned.1.call-update) | async-done | bytes 131088 | tf_op jit(solution)/shard_map/reduce_scatter | solution.py:289
  1030.4 177.4 %reduce-scatter.33.cloned.1.call-done = f32[2048,64]{0,1:T(8,128)} async-done(((f32[2048,1024]{0,1:T(8,128)}), f32[2048,64]{0,1:T(8,128)}) %reduce-scatter.33.cloned.1.call-update) | async-done | bytes 524304 | tf_op jit(solution)/shard_map/reduce_scatter | solution.py:294
  1207.9 183.2 %reduce-scatter.31.cloned.1.call-done = f32[64,2048]{1,0:T(8,128)} async-done(((f32[1024,2048]{1,0:T(8,128)}), f32[64,2048]{1,0:T(8,128)}) %reduce-scatter.31.cloned.1.call-update) | async-done | bytes 524304 | tf_op jit(solution)/shard_map/reduce_scatter | solution.py:293
  1391.1 163.9 %reduce-scatter.35.cloned.1.call-done = f32[96,1024]{1,0:T(8,128)} async-done(((f32[3072,1024]{1,0:T(8,128)}), f32[96,1024]{1,0:T(8,128)}) %reduce-scatter.35.cloned.1.call-update) | async-done | bytes 393232
  (180 shorter events, 63.2 us)
Async XLA Ops:
  7.2 51.3 %copy-start.2 = (bf16[1,512,1024]{2,1,0:T(8,128)(2,1)S(1)}, bf16[1,512,1024]{2,1,0:T(8,128)(2,1)}, u32[]{:S(2)}) copy-start(bf16[1,512,1024]{2,1,0:T(8,128)(2,1)} %param.15) | copy-start | bytes 3145732
  7.2 75.9 %all-gather.12.cloned.1.call-start = ((), (), s32[]{:S(2)}) async-start(), calls=%async_computation.11 | async-start | bytes 6488064 | tf_op jit(solution)/shard_map/all_gather | solution.py:133
  7.9 96.0 %all-gather.14.cloned.1.call-start = ((), (), s32[]{:S(2)}) async-start(), calls=%async_computation.12 | async-start | bytes 6291456 | tf_op jit(solution)/shard_map/all_gather | solution.py:155
  52.6 36.5 %copy-start.28 = (f32[1024]{0:T(1024)}, f32[1024]{0:T(1024)S(1)}, u32[]{:S(2)}) copy-start(f32[1024]{0:T(1024)S(1)} %convert_element_type.166) | copy-start | bytes 12292
  58.7 30.4 %copy-start = (f32[1,512,1024]{2,1,0:T(8,128)}, f32[1,512,1024]{2,1,0:T(8,128)S(1)}, u32[]{:S(2)}) copy-start(f32[1,512,1024]{2,1,0:T(8,128)S(1)} %convert_element_type.164) | copy-start | bytes 6291460
  83.0 5.1 copy-start.6
  89.8 5.5 copy-start.39
  91.6 71.4 %all-gather.18.cloned.1.call-start = ((), (), s32[]{:S(2)}) async-start(), calls=%async_computation.14 | async-start | bytes 1114112 | tf_op jit(solution)/shard_map/all_gather | solution.py:140
  92.3 127.2 %all-gather.20.cloned.1.call-start = ((), (), s32[]{:S(2)}) async-start(), calls=%async_computation.15 | async-start | bytes 1114112 | tf_op jit(solution)/shard_map/all_gather | solution.py:141
  92.9 183.2 %all-gather.16.cloned.1.call-start = ((), (), s32[]{:S(2)}) async-start(), calls=%async_computation.13 | async-start | bytes 1114112 | tf_op jit(solution)/shard_map/all_gather | solution.py:142
  93.5 239.2 %all-gather.22.cloned.1.call-start = ((), (), s32[]{:S(2)}) async-start(), calls=%async_computation.16 | async-start | bytes 1114112 | tf_op jit(solution)/shard_map/all_gather | solution.py:143
  94.0 251.6 %reduce-scatter.15.cloned.1.call-start = ((), (), s32[]{:S(2)}) async-start(), calls=%async_computation.17 | async-start | bytes 3145728 | tf_op jit(solution)/shard_map/reduce_scatter | solution.py:177
  106.7 112.8 %copy-start.21 = (bf16[1,2,512,1024]{3,2,1,0:T(8,128)(2,1)}, bf16[1,2,512,1024]{3,2,1,0:T(8,128)(2,1)S(1)}, u32[]{:S(2)}) copy-start(bf16[1,2,512,1024]{3,2,1,0:T(8,128)(2,1)S(1)} %slice.56) | copy-start | bytes 6291460
  219.5 4.4 copy-start.23
  223.9 16.4 %copy-start.16 = (bf16[2048,512]{0,1:T(8,128)(2,1)}, bf16[2048,512]{0,1:T(8,128)(2,1)S(1)}, u32[]{:S(2)}) copy-start(bf16[2048,512]{0,1:T(8,128)(2,1)S(1)} %convolution_convert_fusion) | copy-start | bytes 6291460
  281.0 15.7 %copy-start.18 = (bf16[2048,512]{0,1:T(8,128)(2,1)}, bf16[2048,512]{0,1:T(8,128)(2,1)S(1)}, u32[]{:S(2)}) copy-start(bf16[2048,512]{0,1:T(8,128)(2,1)S(1)} %convolution_convert_fusion.1) | copy-start | bytes 6291460
  336.8 88.4 %all-gather.26.cloned.1.call-start = ((), (), s32[]{:S(2)}) async-start(), calls=%async_computation.19 | async-start | bytes 4456448 | tf_op jit(solution)/shard_map/all_gather | solution.py:144
  337.6 99.0 %all-gather.24.cloned.1.call-start = ((), (), s32[]{:S(2)}) async-start(), calls=%async_computation.18 | async-start | bytes 3145728 | tf_op jit(solution)/shard_map/all_gather | solution.py:183
  337.7 239.3 %copy-start.26 = (f32[1024]{0:T(1024)}, f32[1024]{0:T(1024)S(1)}, u32[]{:S(2)}) copy-start(f32[1024]{0:T(1024)S(1)} %convert_element_type.177) | copy-start | bytes 12292
  347.2 229.7 %copy-start.32 = (f32[512]{0:T(512)}, f32[512]{0:T(512)S(1)}, u32[]{:S(2)}) copy-start(f32[512]{0:T(512)S(1)} %fusion.66) | copy-start | bytes 6148
  349.8 99.9 %all-gather.30.cloned.1.call-start = ((), (), s32[]{:S(2)}) async-start(), calls=%async_computation.22 | async-start | bytes 3145728 | tf_op jit(solution)/shard_map/all_gather | solution.py:205
  350.4 178.9 %all-gather.28.cloned.1.call-start = ((), (), s32[]{:S(2)}) async-start(), calls=%async_computation.20 | async-start | bytes 4456448 | tf_op jit(solution)/shard_map/all_gather | solution.py:145
  351.2 210.5 %reduce-scatter.19.cloned.1.call-start = ((), (), s32[]{:S(2)}) async-start(), calls=%async_computation.23 | async-start | bytes 3145728 | tf_op jit(solution)/shard_map/reduce_scatter | solution.py:221
  529.3 14.8 copy-start.40
  549.9 21.8 %copy-start.4 = (bf16[1,512,1024]{2,1,0:T(8,128)(2,1)S(1)}, bf16[1,512,1024]{2,1,0:T(8,128)(2,1)}, u32[]{:S(2)}) copy-start(bf16[1,512,1024]{2,1,0:T(8,128)(2,1)} %reduce-scatter.15.cloned.1.call-done) | copy-start | bytes 3145732
  549.9 21.8 %reduce-scatter.17.cloned.1.call-start = ((), (), s32[]{:S(2)}) async-start(), calls=%async_computation.21 | async-start | bytes 3145728 | tf_op jit(solution)/shard_map/reduce_scatter | solution.py:192
  561.1 16.4 %copy-start.11 = (bf16[1,512,1024]{2,1,0:T(8,128)(2,1)S(1)}, bf16[1,512,1024]{2,1,0:T(8,128)(2,1)}, u32[]{:S(2)}) copy-start(bf16[1,512,1024]{2,1,0:T(8,128)(2,1)} %param.29) | copy-start | bytes 3145732
  561.2 30.2 %all-gather.32.cloned.1.call-start = ((), (), s32[]{:S(2)}) async-start(), calls=%async_computation.24 | async-start | bytes 3145728 | tf_op jit(solution)/shard_map/all_gather | solution.py:231
  571.7 5.8 copy-start.13
  579.3 153.2 %reduce-scatter.21.cloned.1.call-start = ((), (), s32[]{:S(2)}) async-start(), calls=%async_computation.25 | async-start | bytes 6291456 | tf_op jit(solution)/shard_map/reduce_scatter | solution.py:274
  594.5 13.8 copy-start.19
  670.3 8.6 copy-start.42
  688.9 124.5 %reduce-scatter.29.cloned.1.call-start = ((), (), s32[]{:S(2)}) async-start(), calls=%async_computation.29 | async-start | bytes 2228224 | tf_op jit(solution)/shard_map/reduce_scatter | solution.py:292
  693.6 174.9 %reduce-scatter.27.cloned.1.call-start = ((), (), s32[]{:S(2)}) async-start(), calls=%async_computation.28 | async-start | bytes 2228224 | tf_op jit(solution)/shard_map/reduce_scatter | solution.py:291
  699.5 7.3 copy-start.22
  699.5 249.9 %reduce-scatter.25.cloned.1.call-start = ((), (), s32[]{:S(2)}) async-start(), calls=%async_computation.27 | async-start | bytes 2228224 | tf_op jit(solution)/shard_map/reduce_scatter | solution.py:290
  706.8 323.7 %reduce-scatter.23.cloned.1.call-start = ((), (), s32[]{:S(2)}) async-start(), calls=%async_computation.26 | async-start | bytes 2228224 | tf_op jit(solution)/shard_map/reduce_scatter | solution.py:289
  709.5 498.4 %reduce-scatter.33.cloned.1.call-start = ((), (), s32[]{:S(2)}) async-start(), calls=%async_computation.31 | async-start | bytes 8912896 | tf_op jit(solution)/shard_map/reduce_scatter | solution.py:294
  721.8 669.3 %reduce-scatter.31.cloned.1.call-start = ((), (), s32[]{:S(2)}) async-start(), calls=%async_computation.30 | async-start | bytes 8912896 | tf_op jit(solution)/shard_map/reduce_scatter | solution.py:293
  732.5 5.0 copy-start.35
  732.5 822.5 %reduce-scatter.35.cloned.1.call-start = ((), (), s32[]{:S(2)}) async-start(), calls=%async_computation.32 | async-start | bytes 12976128
  760.3 7.1 copy-start.38
  760.3 49.4 %copy-start.3 = (bf16[1,512,1024]{2,1,0:T(8,128)(2,1)S(1)}, bf16[1,512,1024]{2,1,0:T(8,128)(2,1)}, u32[]{:S(2)}) copy-start(bf16[1,512,1024]{2,1,0:T(8,128)(2,1)} %param.15) | copy-start | bytes 3145732
  760.3 49.4 %copy-start.5 = (bf16[1,512,1024]{2,1,0:T(8,128)(2,1)S(1)}, bf16[1,512,1024]{2,1,0:T(8,128)(2,1)}, u32[]{:S(2)}) copy-start(bf16[1,512,1024]{2,1,0:T(8,128)(2,1)} %reduce-scatter.15.cloned.1.call-done) | copy-start | bytes 3145732
  760.3 49.4 %copy-start.12 = (bf16[1,512,1024]{2,1,0:T(8,128)(2,1)S(1)}, bf16[1,512,1024]{2,1,0:T(8,128)(2,1)}, u32[]{:S(2)}) copy-start(bf16[1,512,1024]{2,1,0:T(8,128)(2,1)} %param.29) | copy-start | bytes 3145732
  760.3 49.3 %copy-start.27 = (f32[1024]{0:T(1024)S(1)}, f32[1024]{0:T(1024)}, u32[]{:S(2)}) copy-start(f32[1024]{0:T(1024)} %copy-done.26) | copy-start | bytes 12292
  760.3 49.3 %copy-start.33 = (f32[512]{0:T(512)S(1)}, f32[512]{0:T(512)}, u32[]{:S(2)}) copy-start(f32[512]{0:T(512)} %copy-done.32) | copy-start | bytes 6148
  760.3 49.3 %copy-start.37 = (f32[512]{0:T(512)S(1)}, f32[512]{0:T(512)}, u32[]{:S(2)}) copy-start(f32[512]{0:T(512)} %copy-done.36) | copy-start | bytes 6148
  (19 other events, 35.3 us)
Sparse Core Ops, SparseCore 0:
  10.9 72.1 all-gather.11
  91.7 12.1 all-gather.13
  106.7 56.2 all-gather.17
  165.6 53.9 all-gather.19
  222.1 53.8 all-gather.15
  278.7 53.9 all-gather.21
  337.0 8.5 reduce-scatter.14
  348.3 76.8 all-gather.25
  427.4 9.1 all-gather.23
  438.0 11.7 all-gather.29
  452.5 76.7 all-gather.27
  550.0 8.3 reduce-scatter.18
  561.3 10.3 reduce-scatter.16
  579.5 11.8 all-gather.31
  689.0 13.2 reduce-scatter.20
  705.0 82.7 reduce-scatter.28
  790.5 77.9 reduce-scatter.26
  871.2 78.2 reduce-scatter.24
  952.3 78.0 reduce-scatter.22
  1033.2 174.6 reduce-scatter.32
  1210.8 180.2 reduce-scatter.30
  1397.7 157.2 reduce-scatter.34
where the time goes:
time: 1570 us; the launch traced here: 1560 us
  waiting for transfers between devices  1140 us (73%)
  matrix products  209 us (13%)
  blocking collectives  86.5 us (6%)
  other arithmetic  75.1 us (5%)
  local copies, waits for them, and re-layouts  35.8 us (2%)
  between operations  18 us (1%)
    reduce_scatter x1, waiting for transfers between devices, per_device(): lax.psum_scatter(grad_inner_part, 'dp', scatter_dimension=0, tiled=True)  183 us
    reduce_scatter x1, waiting for transfers between devices, per_device(): lax.psum_scatter(grad_outer_part, 'dp', scatter_dimension=1, tiled=True)  177 us
    unnamed x23, waiting for transfers between devices  169 us
    unnamed x3, blocking collectives  86.5 us
    reduce_scatter x1, waiting for transfers between devices, per_device(): lax.psum_scatter(grad_query_part, 'dp', scatter_dimension=0, tiled=True)  81 us
    reduce_scatter x1, waiting for transfers between devices, per_device(): lax.psum_scatter(grad_key_part, 'dp', scatter_dimension=0, tiled=True)  81 us
    all_gather x1, waiting for transfers between devices, per_device(): lax.all_gather(w_outer, 'dp', axis=1, tiled=True)  79.6 us
    all_gather x1, waiting for transfers between devices, per_device(): lax.all_gather(w_inner, 'dp', axis=0, tiled=True)  74.1 us
  transfers between devices with their start and end apart: 22, of which 19 were waited for; matrix products, arithmetic and copies ran while one was open for 11% of the time, Pallas kernels for 0%

commit v1 on v0

--- a/solution.py
+++ b/solution.py
@@ -136,9 +136,24 @@
     )
     gain_attn_f = gain_a_full.astype(jnp.float32)
     gain_ffn_f = gain_f_full.astype(jnp.float32)
+
+    def _try_all_surface(incoming_x, dim_i):
+        parts_n = lax.axis_size("dp")
+        table = tuple(((kk, (kk + 1) % parts_n) for kk in range(parts_n)))
+        panels = tuple(((kk, (kk - 1) % parts_n) for kk in range(parts_n)))
+        right_arr, local_out = ([incoming_x], [incoming_x])
+        for _ in range(parts_n // 2):
+            right_arr.append(lax.ppermute(right_arr[-1], axis_name="dp", perm=table))
+        for _ in range((parts_n - 1) // 2):
+            local_out.append(lax.ppermute(local_out[-1], "dp", perm=panels))
+        small = jnp.concatenate([*right_arr[::-1], *local_out[1:]], dim_i)
+        return jnp.roll(
+            small, (lax.axis_index("dp") - parts_n // 2) * incoming_x.shape[dim_i], dim_i
+        )
+
     query_weight, key_w, value_w, output_weight, inner_weight, outer_weight = (
         lax.all_gather(w_query, "dp", axis=0, tiled=True),
-        lax.all_gather(w_key, "dp", axis=0, tiled=True),
+        _try_all_surface(w_key, 0),
         lax.all_gather(w_value, "dp", axis=0, tiled=True),
         lax.all_gather(w_output, "dp", axis=1, tiled=True),
         lax.all_gather(w_inner, "dp", axis=0, tiled=True),

time: 1570 us -> 1520 us (0.968)
  waiting for transfers between devices: 1140 us -> 1020 us
  starting transfers between devices: 2.01 us -> 44.2 us
  local copies, waits for them, and re-layouts: 35.8 us -> 57.2 us
    all_gather x1, waiting for transfers between devices: 54.7 us -> 0.02 us  [per_device(): lax.all_gather(w_query, 'dp', axis=0, tiled=True)]
    all_gather x1 -> x0, waiting for transfers between devices: 53.1 us -> none  [per_device(): lax.all_gather(w_key, 'dp', axis=0, tiled=True)]
    ppermute x0 -> x15, starting transfers between devices: none -> 43 us  [the longest x7 41.5 us: _try_all_surface(): local_out.append(lax.ppermute(local_out[-1], 'dp', perm=panels))]
    unnamed x98 -> x141, local copies, waits for them, and re-layouts: 27.8 us -> 52 us
    all_gather x1, waiting for transfers between devices: 21.9 us -> 0.02 us  [per_device(): lax.all_gather(w_value, 'dp', axis=0, tiled=True)]
    ppermute x0 -> x15, waiting for transfers between devices: none -> 16.5 us  [the longest x8 8.26 us: _try_all_surface(): right_arr.append(lax.ppermute(right_arr[-1], axis_name='dp', perm=table))]
    unnamed x23 -> x22, waiting for transfers between devices: 169 us -> 168 us
  transfers between devices with their start and end apart: 22 -> 36, of which waited for: 19 -> 22; matrix products, arithmetic and copies ran while one was open for 11% -> 13% of each run, Pallas kernels for 0% -> 0%
where the time goes in v1:
time: 1520 us; the launch traced here: 1510 us
  waiting for transfers between devices  1020 us (67%)
  matrix products  211 us (14%)
  blocking collectives  86.2 us (6%)
  other arithmetic  74.1 us (5%)
  local copies, waits for them, and re-layouts  57.2 us (4%)
  starting transfers between devices  44.2 us (3%)
  between operations  17.8 us (1%)
    reduce_scatter x1, waiting for transfers between devices, per_device(): lax.psum_scatter(grad_inner_part, 'dp', scatter_dimension=0, tiled=True)  183 us
    reduce_scatter x1, waiting for transfers between devices, per_device(): lax.psum_scatter(grad_outer_part, 'dp', scatter_dimension=1, tiled=True)  177 us
    unnamed x22, waiting for transfers between devices  168 us
    unnamed x3, blocking collectives  86.2 us
    reduce_scatter x1, waiting for transfers between devices, per_device(): lax.psum_scatter(grad_key_part, 'dp', scatter_dimension=0, tiled=True)  81 us
    reduce_scatter x1, waiting for transfers between devices, per_device(): lax.psum_scatter(grad_query_part, 'dp', scatter_dimension=0, tiled=True)  80.8 us
    all_gather x1, waiting for transfers between devices, per_device(): lax.all_gather(w_outer, 'dp', axis=1, tiled=True)  79.4 us
    all_gather x1, waiting for transfers between devices, per_device(): lax.all_gather(w_inner, 'dp', axis=0, tiled=True)  75.2 us
  transfers between devices with their start and end apart: 36, of which 22 were waited for; matrix products, arithmetic and copies ran while one was open for 13% of the time, Pallas kernels for 0%

profile of v1, /device:TPU:0, one launch (start us, length us, event | category | flops | bytes accessed | tf_op | source)
XLA Modules:
  0.0 1510.4 jit_solution(10682774808566057533)
XLA Ops:
  9.7 43.0 %all-reduce.6 = (bf16[1024]{0:T(1024)(128)(2,1)S(1)}, bf16[1024]{0:T(1024)(128)(2,1)S(1)}) all-reduce(bf16[1024]{0:T(1024)(128)(2,1)S(1)} %dynamic-update-slice.1, bf16[1024]{0:T(1024)(128)(2,1)S(1)} %dynamic-update-slice), channel_id=1, replica_groups=mesh['dp'=16,'tensor'=2] {'dp','tensor'}, use_global_device_ids=true, to_apply=%add.1 | all-reduce | flops 2048 | bytes 8192
  56.8 26.3 %all-gather.11.cloned.1.call-done = bf16[3072,1024]{1,0:T(8,128)(2,1)} async-done(((bf16[96,1024]{1,0:T(8,128)(2,1)}), bf16[3072,1024]{1,0:T(8,128)(2,1)}) %all-gather.11.cloned.1.call-update) | async-done | bytes 6291472 | tf_op jit(solution)/shard_map/all_gather | solution.py:133
  83.1 5.1 convolution_bitcast_fusion.1
  94.5 6.4 collective-permute-done
  101.0 5.6 collective-permute-start.8
  110.7 5.7 collective-permute-start.9
  118.5 6.1 collective-permute-start.10
  126.5 6.1 collective-permute-start.11
  134.7 6.2 collective-permute-start.12
  143.3 6.1 collective-permute-start.13
  149.4 4.2 fusion.15
  153.6 5.8 collective-permute-start.14
  184.3 7.0 convolution_convert_fusion
  195.2 14.6 fusion.79
  209.9 13.6 fusion
  223.5 4.9 convolution_convert_fusion.1
  228.4 15.7 %fusion.49 = bf16[4,128,1024]{2,1,0:T(8,128)(2,1)} fusion(bf16[2048,4,128]{0,2,1:T(8,128)(2,1)S(1)} %bitcast.131, f32[4,1024,2048]{2,1,0:T(8,128)} %get-tuple-element.112, f32[4,1024]{1,0:T(4,128)S(1)} %fusion, f32[4,1024]{1,0:T(4,128)S(1)} %get-tuple-element.111), kind=kOutput, calls=%fused_computation.82 | convolution fusion | flops 2173173760 | bytes 36732928 | tf_op jit(solution)/shard_map/while/body/eval_jaxpr/hqk,khd->qhd/dot_general | solution.py:52
  244.1 34.5 %all-gather.19.cloned.1.call-done = bf16[512,1024]{0,1:T(8,128)(2,1)} async-done(((bf16[512,64]{0,1:T(8,128)(2,1)}), bf16[512,1024]{0,1:T(8,128)(2,1)}) %all-gather.19.cloned.1.call-update) | async-done | bytes 1048592 | tf_op jit(solution)/shard_map/all_gather | solution.py:158
  283.6 7.9 reduce-scatter.15.cloned.1.call-done
  296.0 75.2 %all-gather.23.cloned.1.call-done = bf16[1024,2048]{1,0:T(8,128)(2,1)} async-done(((bf16[64,2048]{1,0:T(8,128)(2,1)}), bf16[1024,2048]{1,0:T(8,128)(2,1)}) %all-gather.23.cloned.1.call-update) | async-done | bytes 4194320 | tf_op jit(solution)/shard_map/all_gather | solution.py:159
  371.2 11.3 all-gather.21.cloned.1.call-done
  382.5 10.9 fusion.44
  395.9 79.4 %all-gather.25.cloned.1.call-done = bf16[2048,1024]{0,1:T(8,128)(2,1)} async-done(((bf16[2048,64]{0,1:T(8,128)(2,1)}), bf16[2048,1024]{0,1:T(8,128)(2,1)}) %all-gather.25.cloned.1.call-update) | async-done | bytes 4194320 | tf_op jit(solution)/shard_map/all_gather | solution.py:160
  475.3 13.0 fusion.12
  490.4 5.8 convert_bitcast_fusion
  496.2 11.1 convert_bitcast_fusion.1
  507.6 10.3 reduce-scatter.17.cloned.1.call-done
  517.9 5.2 fusion.29
  525.5 11.9 all-gather.29.cloned.1.call-done
  540.6 15.1 %fusion.21 = bf16[4,128,2048]{2,1,0:T(8,128)(2,1)} fusion(bf16[1024,4,128]{0,2,1:T(8,128)(2,1)S(1)} %bitcast.125, f32[4,1024,2048]{2,1,0:T(8,128)} %get-tuple-element.112, f32[4,1024]{1,0:T(4,128)S(1)} %log_add_fusion), kind=kOutput, calls=%fused_computation.43 | convolution fusion | flops 2165309440 | bytes 36716544 | tf_op jit(solution)/shard_map/while/body/eval_jaxpr/hqk,qhd->khd/dot_general | solution.py:61
  555.7 22.0 %multiply_reduce_fusion = (f32[4,1024]{1,0:T(4,128)S(1)}, f32[4,1024,2048]{2,1,0:T(8,128)}) fusion(f32[4,1024,2048]{2,1,0:T(8,128)} %get-tuple-element.112, f32[4,1024]{1,0:T(4,128)S(1)} %log_add_fusion, bf16[1024,4,128]{0,2,1:T(8,128)(2,1)S(1)} %bitcast.126, bf16[2048,4,128]{0,2,1:T(8,128)(2,1)S(1)} %bitcast.132), kind=kOutput, calls=%fused_computation.1 | convolution fusion | flops 2172645376 | bytes 70287360 | tf_op jit(solution)/shard_map/while/body/eval_jaxpr/qhd,khd->hqk/dot_general | solution.py:60
  577.7 28.2 %multiply_convert_fusion = bf16[4,1024,2048]{2,1,0:T(8,128)(2,1)} fusion(f32[4,1024,2048]{2,1,0:T(8,128)} %get-tuple-element.114, f32[4,1024,2048]{2,1,0:T(8,128)} %get-tuple-element.112, f32[4,1024]{1,0:T(4,128)S(1)} %get-tuple-element.113, f32[4,1024]{1,0:T(4,128)S(1)} %log_add_fusion), kind=kLoop, calls=%fused_computation | loop fusion | flops 33554432 | bytes 83918848 | tf_op jit(solution)/shard_map/while/body/eval_jaxpr/convert_element_type | solution.py:66
  606.0 11.4 multiply_convert_fusion.4
  617.4 8.7 multiply_convert_fusion.2
  637.5 4.5 fusion.32
  642.2 6.8 fusion.74
  649.1 6.1 fusion.75
  661.0 11.3 fusion.36
  673.9 9.0 fusion.42
  691.7 6.4 convolution_bitcast_fusion
  698.2 12.7 copy.41
  717.9 40.8 %all-reduce.5 = (f32[1024]{0:T(1024)S(1)}, f32[1024]{0:T(1024)S(1)}) all-reduce(f32[1024]{0:T(1024)S(1)} %get-tuple-element.93, f32[1024]{0:T(1024)S(1)} %copy-done.43), channel_id=11, replica_groups=mesh['dp'=16,'tensor'=2] {'dp','tensor'}, use_global_device_ids=true, to_apply=%region_17.18.clone | all-reduce | flops 2048 | bytes 16384
  763.6 53.5 %reduce-scatter.27.cloned.1.call-done = f32[64,512]{1,0:T(8,128)} async-done(((f32[1024,512]{1,0:T(8,128)}), f32[64,512]{1,0:T(8,128)}) %reduce-scatter.27.cloned.1.call-update) | async-done | bytes 131088 | tf_op jit(solution)/shard_map/reduce_scatter | solution.py:306
  817.1 81.0 %reduce-scatter.25.cloned.1.call-done = f32[64,512]{1,0:T(8,128)} async-done(((f32[1024,512]{1,0:T(8,128)}), f32[64,512]{1,0:T(8,128)}) %reduce-scatter.25.cloned.1.call-update) | async-done | bytes 131088 | tf_op jit(solution)/shard_map/reduce_scatter | solution.py:305
  898.1 80.8 %reduce-scatter.23.cloned.1.call-done = f32[64,512]{1,0:T(8,128)} async-done(((f32[1024,512]{1,0:T(8,128)}), f32[64,512]{1,0:T(8,128)}) %reduce-scatter.23.cloned.1.call-update) | async-done | bytes 131088 | tf_op jit(solution)/shard_map/reduce_scatter | solution.py:304
  979.0 177.3 %reduce-scatter.33.cloned.1.call-done = f32[2048,64]{0,1:T(8,128)} async-done(((f32[2048,1024]{0,1:T(8,128)}), f32[2048,64]{0,1:T(8,128)}) %reduce-scatter.33.cloned.1.call-update) | async-done | bytes 524304 | tf_op jit(solution)/shard_map/reduce_scatter | solution.py:309
  1156.3 183.0 %reduce-scatter.31.cloned.1.call-done = f32[64,2048]{1,0:T(8,128)} async-done(((f32[1024,2048]{1,0:T(8,128)}), f32[64,2048]{1,0:T(8,128)}) %reduce-scatter.31.cloned.1.call-update) | async-done | bytes 524304 | tf_op jit(solution)/shard_map/reduce_scatter | solution.py:308
  1339.4 164.0 %reduce-scatter.35.cloned.1.call-done = f32[96,1024]{1,0:T(8,128)} async-done(((f32[3072,1024]{1,0:T(8,128)}), f32[96,1024]{1,0:T(8,128)}) %reduce-scatter.35.cloned.1.call-update) | async-done | bytes 393232
  (251 shorter events, 111.1 us)
Async XLA Ops:
  7.2 47.7 %copy-start.25 = (bf16[1,768,1024]{2,1,0:T(8,128)(2,1)S(1)}, bf16[1,768,1024]{2,1,0:T(8,128)(2,1)}, u32[]{:S(2)}) copy-start(bf16[1,768,1024]{2,1,0:T(8,128)(2,1)} %param.17) | copy-start | bytes 4718596
  7.2 75.9 %all-gather.11.cloned.1.call-start = ((), (), s32[]{:S(2)}) async-start(), calls=%async_computation.11 | async-start | bytes 6488064 | tf_op jit(solution)/shard_map/all_gather | solution.py:133
  7.9 171.6 %all-gather.13.cloned.1.call-start = ((), (), s32[]{:S(2)}) async-start(), calls=%async_computation.12 | async-start | bytes 6291456 | tf_op jit(solution)/shard_map/all_gather | solution.py:170
  52.7 36.5 %copy-start.33 = (f32[1024]{0:T(1024)}, f32[1024]{0:T(1024)S(1)}, u32[]{:S(2)}) copy-start(f32[1024]{0:T(1024)S(1)} %convert_element_type.166) | copy-start | bytes 12292
  56.8 32.5 %copy-start = (f32[1,512,1024]{2,1,0:T(8,128)}, f32[1,512,1024]{2,1,0:T(8,128)S(1)}, u32[]{:S(2)}) copy-start(f32[1,512,1024]{2,1,0:T(8,128)S(1)} %convert_element_type.164) | copy-start | bytes 6291460
  91.7 99.6 %all-gather.17.cloned.1.call-start = ((), (), s32[]{:S(2)}) async-start(), calls=%async_computation.14 | async-start | bytes 1114112 | tf_op jit(solution)/shard_map/all_gather | solution.py:155
  92.4 131.1 %all-gather.15.cloned.1.call-start = ((), (), s32[]{:S(2)}) async-start(), calls=%async_computation.13 | async-start | bytes 1114112 | tf_op jit(solution)/shard_map/all_gather | solution.py:157
  93.0 185.6 %all-gather.19.cloned.1.call-start = ((), (), s32[]{:S(2)}) async-start(), calls=%async_computation.15 | async-start | bytes 1114112 | tf_op jit(solution)/shard_map/all_gather | solution.py:158
  93.0 7.9 collective-permute-start
  101.0 7.9 collective-permute-start.1
  101.0 9.8 collective-permute-start.8
  106.6 184.9 %reduce-scatter.15.cloned.1.call-start = ((), (), s32[]{:S(2)}) async-start(), calls=%async_computation.16 | async-start | bytes 3145728 | tf_op jit(solution)/shard_map/reduce_scatter | solution.py:192
  108.8 7.9 collective-permute-start.2
  110.7 7.7 collective-permute-start.9
  116.7 7.9 collective-permute-start.3
  118.5 8.1 collective-permute-start.10
  124.6 8.0 collective-permute-start.4
  126.5 8.1 collective-permute-start.11
  132.6 8.2 collective-permute-start.5
  134.7 8.6 collective-permute-start.12
  140.8 8.6 collective-permute-start.6
  143.3 10.3 collective-permute-start.13
  149.4 9.9 collective-permute-start.7
  153.6 15.2 %collective-permute-start.14 = (bf16[64,512]{1,0:T(8,128)(2,1)S(1)}, bf16[64,512]{1,0:T(8,128)(2,1)S(1)}, u32[]{:S(2)}, u32[]{:S(2)}) collective-permute-start(bf16[64,512]{1,0:T(8,128)(2,1)S(1)} %collective-permute-done.13), channel_id=1, source_target_pairs={{0,30},{2,0},{4,2},{6,4},{8,6},{10,8},{12,10},{14,12},{16,14},{18,... | collective-permute-start | bytes 196616 | tf_op jit(solution)/shard_map/ppermute | solution.py:148
  282.8 88.4 %all-gather.23.cloned.1.call-start = ((), (), s32[]{:S(2)}) async-start(), calls=%async_computation.18 | async-start | bytes 4456448 | tf_op jit(solution)/shard_map/all_gather | solution.py:159
  283.5 99.0 %all-gather.21.cloned.1.call-start = ((), (), s32[]{:S(2)}) async-start(), calls=%async_computation.17 | async-start | bytes 3145728 | tf_op jit(solution)/shard_map/all_gather | solution.py:198
  283.6 239.5 %copy-start.31 = (f32[1024]{0:T(1024)}, f32[1024]{0:T(1024)S(1)}, u32[]{:S(2)}) copy-start(f32[1024]{0:T(1024)S(1)} %convert_element_type.177) | copy-start | bytes 12292
  293.3 229.8 %copy-start.37 = (f32[512]{0:T(512)}, f32[512]{0:T(512)S(1)}, u32[]{:S(2)}) copy-start(f32[512]{0:T(512)S(1)} %fusion.68) | copy-start | bytes 6148
  294.7 101.2 %all-gather.27.cloned.1.call-start = ((), (), s32[]{:S(2)}) async-start(), calls=%async_computation.21 | async-start | bytes 3145728 | tf_op jit(solution)/shard_map/all_gather | solution.py:220
  295.4 179.9 %all-gather.25.cloned.1.call-start = ((), (), s32[]{:S(2)}) async-start(), calls=%async_computation.19 | async-start | bytes 4456448 | tf_op jit(solution)/shard_map/all_gather | solution.py:160
  296.0 211.6 %reduce-scatter.19.cloned.1.call-start = ((), (), s32[]{:S(2)}) async-start(), calls=%async_computation.22 | async-start | bytes 3145728 | tf_op jit(solution)/shard_map/reduce_scatter | solution.py:236
  496.2 21.7 %reduce-scatter.17.cloned.1.call-start = ((), (), s32[]{:S(2)}) async-start(), calls=%async_computation.20 | async-start | bytes 3145728 | tf_op jit(solution)/shard_map/reduce_scatter | solution.py:207
  507.3 30.1 %all-gather.29.cloned.1.call-start = ((), (), s32[]{:S(2)}) async-start(), calls=%async_computation.23 | async-start | bytes 3145728 | tf_op jit(solution)/shard_map/all_gather | solution.py:246
  525.5 157.5 %reduce-scatter.21.cloned.1.call-start = ((), (), s32[]{:S(2)}) async-start(), calls=%async_computation.24 | async-start | bytes 6291456 | tf_op jit(solution)/shard_map/reduce_scatter | solution.py:289
  577.7 28.2 %copy-start.17 = (bf16[2048,512]{0,1:T(8,128)(2,1)S(1)}, bf16[2048,512]{0,1:T(8,128)(2,1)}, u32[]{:S(2)}) copy-start(bf16[2048,512]{0,1:T(8,128)(2,1)} %copy-done.16) | copy-start | bytes 6291460
  637.5 126.1 %reduce-scatter.29.cloned.1.call-start = ((), (), s32[]{:S(2)}) async-start(), calls=%async_computation.28 | async-start | bytes 2228224 | tf_op jit(solution)/shard_map/reduce_scatter | solution.py:307
  642.1 175.0 %reduce-scatter.27.cloned.1.call-start = ((), (), s32[]{:S(2)}) async-start(), calls=%async_computation.27 | async-start | bytes 2228224 | tf_op jit(solution)/shard_map/reduce_scatter | solution.py:306
  649.0 249.1 %reduce-scatter.25.cloned.1.call-start = ((), (), s32[]{:S(2)}) async-start(), calls=%async_computation.26 | async-start | bytes 2228224 | tf_op jit(solution)/shard_map/reduce_scatter | solution.py:305
  655.2 323.8 %reduce-scatter.23.cloned.1.call-start = ((), (), s32[]{:S(2)}) async-start(), calls=%async_computation.25 | async-start | bytes 2228224 | tf_op jit(solution)/shard_map/reduce_scatter | solution.py:304
  659.4 496.9 %reduce-scatter.33.cloned.1.call-start = ((), (), s32[]{:S(2)}) async-start(), calls=%async_computation.30 | async-start | bytes 8912896 | tf_op jit(solution)/shard_map/reduce_scatter | solution.py:309
  672.4 667.0 %reduce-scatter.31.cloned.1.call-start = ((), (), s32[]{:S(2)}) async-start(), calls=%async_computation.29 | async-start | bytes 8912896 | tf_op jit(solution)/shard_map/reduce_scatter | solution.py:308
  682.9 820.4 %reduce-scatter.35.cloned.1.call-start = ((), (), s32[]{:S(2)}) async-start(), calls=%async_computation.31 | async-start | bytes 12976128
  710.9 49.0 %copy-start.3 = (bf16[1,512,1024]{2,1,0:T(8,128)(2,1)S(1)}, bf16[1,512,1024]{2,1,0:T(8,128)(2,1)}, u32[]{:S(2)}) copy-start(bf16[1,512,1024]{2,1,0:T(8,128)(2,1)} %param.15) | copy-start | bytes 3145732
  710.9 49.0 %copy-start.5 = (bf16[1,512,1024]{2,1,0:T(8,128)(2,1)S(1)}, bf16[1,512,1024]{2,1,0:T(8,128)(2,1)}, u32[]{:S(2)}) copy-start(bf16[1,512,1024]{2,1,0:T(8,128)(2,1)} %reduce-scatter.15.cloned.1.call-done) | copy-start | bytes 3145732
  710.9 49.0 %copy-start.12 = (bf16[1,512,1024]{2,1,0:T(8,128)(2,1)S(1)}, bf16[1,512,1024]{2,1,0:T(8,128)(2,1)}, u32[]{:S(2)}) copy-start(bf16[1,512,1024]{2,1,0:T(8,128)(2,1)} %param.29) | copy-start | bytes 3145732
  710.9 49.0 %copy-start.32 = (f32[1024]{0:T(1024)S(1)}, f32[1024]{0:T(1024)}, u32[]{:S(2)}) copy-start(f32[1024]{0:T(1024)} %copy-done.31) | copy-start | bytes 12292
  710.9 49.0 %copy-start.38 = (f32[512]{0:T(512)S(1)}, f32[512]{0:T(512)}, u32[]{:S(2)}) copy-start(f32[512]{0:T(512)} %copy-done.37) | copy-start | bytes 6148
  710.9 49.0 %copy-start.42 = (f32[512]{0:T(512)S(1)}, f32[512]{0:T(512)}, u32[]{:S(2)}) copy-start(f32[512]{0:T(512)} %copy-done.41) | copy-start | bytes 6148
  (39 other events, 187.6 us)
Sparse Core Ops, SparseCore 0:
  10.9 72.2 all-gather.10
  91.8 12.1 all-gather.12
  106.8 57.2 all-gather.16
  166.7 55.2 all-gather.14
  224.6 53.9 all-gather.18
  282.9 8.5 reduce-scatter.14
  294.3 76.8 all-gather.22
  373.3 9.1 all-gather.20
  384.1 11.7 all-gather.26
  398.5 76.7 all-gather.24
  496.3 8.3 reduce-scatter.18
  507.4 10.3 reduce-scatter.16
  525.6 11.8 all-gather.28
  637.6 13.2 reduce-scatter.20
  653.6 82.7 reduce-scatter.28
  739.0 78.0 reduce-scatter.26
  819.8 78.2 reduce-scatter.24
  900.8 78.0 reduce-scatter.22
  981.9 174.4 reduce-scatter.32
  1159.0 180.2 reduce-scatter.30
  1346.0 157.3 reduce-scatter.34
